TPU v7x, 32 devices: a whole 2x2x4 slice. The times are simulated.
32 devices in a mesh: groups: 2 (over y), feat: 4 (over z), layer: 2 (over x), row: 2 (over core).
Axes of the slice: x: 2, y: 2, z: 4, core: 2. Of those that a mesh axis runs over, the one named last changes fastest.
Arguments:
- resid_buf: bfloat16 [512, 2, 4608], P(('groups', 'feat', 'row')), parts along dimension 0, may hold values from -6 to 6
- shuffle: int32 [512], P('groups'), parts along dimension 0, may hold values from 0 to 255, each once
- mlp_out: bfloat16 [512, 2, 4608], P(('groups', 'feat', 'row')), parts along dimension 0, may hold values from -5 to 5
- enc_weight: bfloat16 [2, 8192, 4608], P('layer', 'feat', 'row'), may hold values from -0.09375 to 0.09375
- dec_weight: bfloat16 [2, 8192, 2, 4608], P('layer', 'feat', None, 'row'), may hold values from -0.0625 to 0.0625
- enc_bias: float32 [2, 8192], P('layer', 'feat'), may hold values from -0.5 to 0.5
- dec_bias: float32 [2, 4608], replicated, may hold values from -3 to 3
Outputs:
- rebuilt: bfloat16 [512, 2, 4608], P(('groups', 'feat', 'row')), parts along dimension 0
- enc_grad: bfloat16 [4, 8192, 4608], P(('groups', 'layer'), 'feat', 'row'), parts along dimension 0
- dec_grad: bfloat16 [4, 8192, 2, 4608], P(('groups', 'layer'), 'feat', None, 'row'), parts along dimension 0
- bias_grad: float32 [4, 8192], P(('groups', 'layer'), 'feat'), parts along dimension 0
There are 2 independent parts, one for each index of `groups`. A program takes and returns all parts, laid end to end along the dimension named above; an argument that names none is the same for every part. Nothing has to cross between parts.
Inputs may be any that keep to these rules, and one draw needn't show every extreme that they name: `shuffle`: a permutation of the 256 buffer rows.
All inputs are finite; a program needn't handle non-finite values.
Results may differ from a plain program's by a relative error of at most 0.04.
Values may be sent and summed in bfloat16 or wider, within the bound.
A program may use at most 128 MiB of HBM per device.

v0:
```python
import jax
import jax.numpy as jnp
from jax import lax
from jax.sharding import PartitionSpec as P

LAYERS = 2


def from_behind(block, axis, distance):
    devices = range(lax.axis_size(axis))
    route = [(i - distance, i) for i in devices if i - distance in devices]
    return lax.ppermute(block, axis, route)


def dot_last(left, right):
    return lax.dot_general(
        left, right, (((1,), (1,)), ((), ())), preferred_element_type=jnp.float32
    )


def dot_first(left, right):
    return lax.dot_general(
        left, right, (((0,), (0,)), ((), ())), preferred_element_type=jnp.float32
    )


def on_device(resid_buf, shuffle, mlp_out, enc_weight, dec_weight, enc_bias, dec_bias):
    feat_count = lax.axis_size("feat")
    row_count = lax.axis_size("row")
    sub_blocks = lax.axis_size("layer") // LAYERS
    layer_pos = lax.axis_index("layer")
    row_pos = lax.axis_index("row")
    source = layer_pos // sub_blocks
    rows_each = resid_buf.shape[0]
    width = dec_bias.shape[1]
    half_width = enc_weight.shape[2]
    local_rows = rows_each * feat_count
    total_rows = local_rows * row_count
    loss_scale = float(total_rows) ** (-0.5)
    own_layer = lax.dynamic_index_in_dim(resid_buf, source, axis=1, keepdims=False)
    buffer_all = lax.all_gather(own_layer, ("feat", "row"), axis=0, tiled=True)
    batch_rows = jnp.take(buffer_all, shuffle, axis=0)
    blocks = batch_rows.reshape(feat_count, row_count, rows_each, width)
    inputs_half = lax.dynamic_slice_in_dim(
        jnp.swapaxes(blocks, 0, 1), row_pos * half_width, half_width, axis=3
    )
    inputs_half = inputs_half.reshape(total_rows, half_width)
    own_half_dec = dec_weight[0][:, 0]
    next_half_dec = dec_weight[0][:, 1]
    pre_all = lax.psum(dot_last(inputs_half, enc_weight[0]), "row") + enc_bias[0]
    features_all = jnp.maximum(pre_all, 0.0).astype(jnp.bfloat16)
    own_part = jnp.dot(features_all, own_half_dec, preferred_element_type=jnp.float32)
    next_part = jnp.dot(features_all, next_half_dec, preferred_element_type=jnp.float32)
    carried = from_behind(next_part, "layer", sub_blocks)
    spread = (own_part + carried).reshape(row_count, local_rows, half_width)
    halves = lax.psum_scatter(spread, "feat", scatter_dimension=1, tiled=True)
    joined = lax.all_to_all(halves, "row", split_axis=0, concat_axis=2, tiled=True)
    section_sum = joined.reshape(rows_each, width)
    target_ids = jnp.arange(LAYERS, dtype=jnp.int32)
    target_slots = jnp.where((target_ids == source)[:, None, None], section_sum[None], 0.0)
    totals = lax.psum(target_slots, "layer")
    recon_sum = jnp.swapaxes(totals, 0, 1) + dec_bias[None]
    errors = (recon_sum - mlp_out.astype(jnp.float32)).astype(jnp.bfloat16)
    gathered = lax.all_gather(errors, ("feat", "row"), axis=0, tiled=True)
    error_grid = gathered.reshape(feat_count, row_count, rows_each, LAYERS, width)
    errors_mine = lax.dynamic_index_in_dim(error_grid, row_pos, axis=1, keepdims=False)
    errors_mine = errors_mine.reshape(local_rows, LAYERS, width)
    errors_half = lax.dynamic_slice_in_dim(
        jnp.swapaxes(error_grid, 0, 1), row_pos * half_width, half_width, axis=4
    )
    errors_half = errors_half.reshape(total_rows, LAYERS, half_width)
    live_next = source + 1 < LAYERS
    next_index = jnp.minimum(source + 1, LAYERS - 1)
    half_own = lax.dynamic_index_in_dim(errors_half, source, axis=1, keepdims=False)
    half_next = lax.dynamic_index_in_dim(errors_half, next_index, axis=1, keepdims=False)
    half_next = jnp.where(live_next, half_next, jnp.zeros_like(half_next))
    half_terms = dot_last(half_own, own_half_dec) + dot_last(half_next, next_half_dec)
    grad_feats = lax.psum(half_terms, "row") * loss_scale
    grad_all = jnp.where(pre_all > 0, grad_feats, 0.0).astype(jnp.bfloat16)
    grad_own = loss_scale * dot_first(features_all, half_own)
    grad_next = loss_scale * dot_first(features_all, half_next)
    enc_grad = dot_first(grad_all, inputs_half).astype(jnp.bfloat16)
    dec_grad = jnp.stack([grad_own, grad_next], axis=1).astype(jnp.bfloat16)
    bias_grad = jnp.sum(grad_all.astype(jnp.float32), axis=0)
    return (recon_sum.astype(jnp.bfloat16), enc_grad[None], dec_grad[None], bias_grad[None])


def solution(mesh):
    return jax.shard_map(
        on_device,
        mesh=mesh,
        in_specs=(
            P(("groups", "feat", "row"), None, None),
            P("groups"),
            P(("groups", "feat", "row"), None, None),
            P("layer", "feat", "row"),
            P("layer", "feat", None, "row"),
            P("layer", "feat"),
            P(),
        ),
        out_specs=(
            P(("groups", "feat", "row"), None, None),
            P(("groups", "layer"), "feat", "row"),
            P(("groups", "layer"), "feat", None, "row"),
            P(("groups", "layer"), "feat"),
        ),
        check_vma=False,
    )
```

profile of v0, /device:TPU:0, one launch (start us, length us, event | category | flops | bytes accessed | tf_op | source)
XLA Modules:
  0.0 529.7 jit_solution(15762774988231695739)
XLA Ops:
  7.2 1.0 copy-done
  8.2 0.6 constant_dynamic-slice_fusion.1
  8.9 0.7 copy.39
  9.8 34.6 %all-gather.6.cloned.1.call-done = bf16[256,1,4608]{2,0,1:T(8,128)(2,1)} async-done(((bf16[32,1,4608]{2,0,1:T(8,128)(2,1)}), bf16[256,1,4608]{2,0,1:T(8,128)(2,1)}) %all-gather.6.cloned.1.call-update) | async-done | bytes 2359312 | tf_op jit(solution)/shard_map/all_gather | solution.py:41
  44.4 6.3 %gather_fusion = bf16[256,4608]{1,0:T(8,128)(2,1)S(1)} fusion(bf16[256,4608]{1,0:T(8,128)(2,1)} %bitcast.65, s32[1024]{0:T(1024)S(1)} %pad_clamp_fusion), kind=kCustom, calls=%fused_computation | custom fusion | bytes 4719616 | tf_op jit(solution)/shard_map/jit(_take)/gather | solution.py:42
  51.0 1.0 copy-done.4
  52.0 7.6 %fusion.3 = f32[256,2048]{1,0:T(8,128)} fusion(bf16[256,2304]{1,0:T(8,128)(2,1)S(1)} %bitcast.71, bf16[1,2048,2304]{2,1,0:T(8,128)(2,1)} %param.10), kind=kOutput, calls=%fused_computation.11 | convolution fusion | flops 2415919104 | bytes 12713984 | tf_op jit(solution)/shard_map/dot_general | solution.py:16
  59.7 18.2 %copy.45 = bf16[1,2048,2,2304]{3,1,2,0:T(8,128)(2,1)} copy(bf16[1,2048,2,2304]{3,2,1,0:T(2,128)(2,1)} %param.11) | data formatting | bytes 37748736 | tf_op args[4]
  77.9 2.4 all-reduce.6.cloned.1.call-done
  80.4 2.0 maximum_convert_fusion
  82.3 6.6 %fusion.8 = f32[256,2304]{1,0:T(8,128)S(1)} fusion(bf16[256,2048]{1,0:T(8,128)(2,1)S(1)} %maximum_convert_fusion, bf16[2048,2,2304]{2,0,1:T(8,128)(2,1)} %bitcast.66), kind=kOutput, calls=%fused_computation.16 | convolution fusion | flops 2415919104 | bytes 12845056 | tf_op jit(solution)/shard_map/dot_general | solution.py:53
  89.0 4.1 collective-permute-start
  93.1 50.6 %collective-permute-done = f32[256,2304]{1,0:T(8,128)S(1)} collective-permute-done((f32[256,2304]{1,0:T(8,128)S(1)}, f32[256,2304]{1,0:T(8,128)S(1)}, u32[]{:S(2)}, u32[]{:S(2)}) %collective-permute-start) | collective-permute-done | bytes 2359328 | tf_op jit(solution)/shard_map/ppermute | solution.py:12
  143.7 2.7 fusion.9
  146.4 3.2 copy.32
  151.5 94.8 %all-reduce.12.cloned.1.call-done = f32[2,128,2304]{2,0,1:T(2,128)} async-done(((f32[2,128,2304]{2,0,1:T(2,128)}), f32[2,128,2304]{2,0,1:T(2,128)}) %all-reduce.12.cloned.1.call-update) | async-done | bytes 2359312
  246.4 1.1 constant_dynamic-slice_fusion.2
  247.5 4.2 all_to_all.15
  252.3 1.2 broadcast_select_fusion
  253.5 42.1 %all-reduce.8.cloned.1.call-done = f32[2,32,4608]{2,1,0:T(8,128)} async-done(((f32[2,32,4608]{2,1,0:T(8,128)}), f32[2,32,4608]{2,1,0:T(8,128)}) %all-reduce.8.cloned.1.call-update) | async-done | bytes 1179664 | tf_op jit(solution)/shard_map/psum | solution.py:61
  295.6 2.5 fusion.15
  298.2 1.4 copy.37
  299.7 49.8 %all-gather.4.cloned.1.call-done = bf16[256,2,4608]{2,0,1:T(8,128)(2,1)} async-done(((bf16[32,2,4608]{2,0,1:T(8,128)(2,1)}), bf16[256,2,4608]{2,0,1:T(8,128)(2,1)}) %all-gather.4.cloned.1.call-update) | async-done | bytes 4718608 | tf_op jit(solution)/shard_map/all_gather | solution.py:64
  349.4 1.9 dynamic-slice_bitcast_fusion
  351.5 6.1 %fusion.5 = f32[256,2048]{1,0:T(8,128)S(1)} fusion(bf16[2048,2,2304]{2,0,1:T(8,128)(2,1)} %bitcast.67, bf16[256,2,2304]{2,0,1:T(8,128)(2,1)S(1)} %bitcast.73, s32[]{:T(128)S(6)} %select_n.47), kind=kOutput, calls=%fused_computation.13 | convolution fusion | flops 2415919104 | bytes 12713988 | tf_op jit(solution)/shard_map/dot_general | solution.py:16
  357.6 7.7 %fusion.10 = f32[256,2048]{1,0:T(8,128)} fusion(f32[256,2048]{1,0:T(8,128)S(1)} %fusion.5, bf16[2048,2,2304]{2,0,1:T(8,128)(2,1)} %bitcast.68, bf16[256,2,2304]{2,0,1:T(8,128)(2,1)S(1)} %bitcast.74, s32[]{:T(128)S(6)} %select_n.52, pred[]{:T(512)S(6)} %lt.28), kind=kOutput, calls=%fused_computation.18 | convolution fusion | flops 2417033216 | bytes 14811141 | tf_op jit(solution)/shard_map/dot_general | solution.py:16
  365.3 4.4 fusion.1
  369.7 5.2 fusion.2
  374.9 7.4 %pad_maximum_fusion = bf16[1,2048,2,2304]{3,1,2,0:T(8,128)(2,1)S(1)} fusion(bf16[1,2048,1,2304]{3,1,2,0:T(8,128)(2,1)} %fusion.2, bf16[1,2048,1,2304]{3,1,2,0:T(8,128)(2,1)S(1)} %fusion.1), kind=kLoop, calls=%fused_computation.1 | loop fusion | flops 9437184 | bytes 37748736 | tf_op jit(solution)/shard_map/stack | solution.py:83
  382.3 132.7 %copy.38 = bf16[1,2048,2,2304]{3,2,1,0:T(2,128)(2,1)} copy(bf16[1,2048,2,2304]{3,1,2,0:T(8,128)(2,1)S(1)} %pad_maximum_fusion) | data formatting | bytes 37748736
  515.0 2.7 convert_reduce_fusion
  517.7 5.2 fusion
  (50 shorter events, 2.7 us)
Async XLA Ops:
  7.2 1.1 copy-start
  7.2 2.5 copy-start.11
  7.2 37.2 %all-gather.6.cloned.1.call-start = ((), (), s32[]{:S(2)}) async-start(), calls=%async_computation.5 | async-start | bytes 2654208 | tf_op jit(solution)/shard_map/all_gather | solution.py:41
  9.6 70.7 %all-reduce.6.cloned.1.call-start = ((), (), s32[]{:S(2)}) async-start(), calls=%async_computation.1 | async-start | bytes 4194304 | tf_op jit(solution)/shard_map/psum | solution.py:50
  51.0 1.0 copy-start.4
  59.7 20.7 %copy-start.10 = (f32[1,2048]{1,0:T(1,128)S(1)}, f32[1,2048]{1,0:T(1,128)}, u32[]{:S(2)}) copy-start(f32[1,2048]{1,0:T(1,128)} %param.12) | copy-start | bytes 24580
  59.7 186.7 %all-reduce.12.cloned.1.call-start = ((), (), s32[]{:S(2)}) async-start(), calls=%async_computation.6 | async-start | bytes 4718592
  80.4 63.3 %copy-start.2 = (bf16[1,2048,2,2304]{3,1,2,0:T(8,128)(2,1)S(1)}, bf16[1,2048,2,2304]{3,1,2,0:T(8,128)(2,1)}, u32[]{:S(2)}) copy-start(bf16[1,2048,2,2304]{3,1,2,0:T(8,128)(2,1)} %copy.45) | copy-start | bytes 56623108
  89.0 54.7 %collective-permute-start = (f32[256,2304]{1,0:T(8,128)S(1)}, f32[256,2304]{1,0:T(8,128)S(1)}, u32[]{:S(2)}, u32[]{:S(2)}) collective-permute-start(f32[256,2304]{1,0:T(8,128)S(1)} %fusion.8), channel_id=1, source_target_pairs={{0,2},{1,3},{4,6},{5,7},{8,10},{9,11},{12,14},{13,15},{16,18},{17,... | collective-permute-start | bytes 7077896 | tf_op jit(solution)/shard_map/ppermute | solution.py:12
  149.6 0.7 copy-start.12
  149.7 145.9 %all-reduce.8.cloned.1.call-start = ((), (), s32[]{:S(2)}) async-start(), calls=%async_computation.2 | async-start | bytes 2359296 | tf_op jit(solution)/shard_map/psum | solution.py:61
  252.2 43.4 %copy-start.9 = (f32[2,4608]{1,0:T(2,128)S(1)}, f32[2,4608]{1,0:T(2,128)}, u32[]{:S(2)}) copy-start(f32[2,4608]{1,0:T(2,128)} %param.13) | copy-start | bytes 110596
  253.4 96.0 %all-gather.4.cloned.1.call-start = ((), (), s32[]{:S(2)}) async-start(), calls=%async_computation.3 | async-start | bytes 5308416 | tf_op jit(solution)/shard_map/all_gather | solution.py:64
  295.6 2.6 copy-start.6
  298.1 216.9 %all-reduce.10.cloned.1.call-start = ((), (), s32[]{:S(2)}) async-start(), calls=%async_computation.4 | async-start | bytes 4194304 | tf_op jit(solution)/shard_map/psum | solution.py:78
  351.5 6.1 %copy-start.7 = (bf16[2,4,32,2,2304]{4,2,1,0,3:T(8,128)(2,1)}, bf16[2,4,32,2,2304]{4,2,1,0,3:T(8,128)(2,1)S(1)}, u32[]{:S(2)}) copy-start(bf16[2,4,32,2,2304]{4,2,1,0,3:T(8,128)(2,1)S(1)} %copy.36) | copy-start | bytes 7077892
  365.3 4.4 copy-start.8
  382.3 132.7 %copy-start.3 = (f32[256,2048]{1,0:T(8,128)S(1)}, f32[256,2048]{1,0:T(8,128)}, u32[]{:S(2)}) copy-start(f32[256,2048]{1,0:T(8,128)} %all-reduce.6.cloned.1.call-done) | copy-start | bytes 6291460
  515.0 2.7 copy-start.5
  517.7 5.2 copy-start.1
Sparse Core Ops, SparseCore 0:
  10.2 34.1 all-gather.5
  59.8 20.5 all-reduce.5
  149.8 96.5 all-reduce.11
  253.6 41.9 all-reduce.7
  298.2 51.1 all-gather.3
  365.4 20.0 all-reduce.9
where the time goes:
time: 530 us
  waiting for transfers between devices  274 us (52%)
  local copies, waits for them, and re-layouts  170 us (32%)
  matrix products  45.5 us (9%)
  other arithmetic  16.1 us (3%)
  between operations  15 us (3%)
    unnamed x33, local copies, waits for them, and re-layouts  157 us
    unnamed x7, waiting for transfers between devices  94.9 us
    ppermute x1, waiting for transfers between devices, from_behind(): return lax.ppermute(block, axis, route)  50.6 us
    all_gather x1, waiting for transfers between devices, on_device(): gathered = lax.all_gather(errors, ('feat', 'row'), axis=0, tiled=True)  49.8 us
    psum x1, waiting for transfers between devices, on_device(): totals = lax.psum(target_slots, 'layer')  42.1 us
    all_gather x1, waiting for transfers between devices, on_device(): buffer_all = lax.all_gather(own_layer, ('feat', 'row'), axis=0, tiled=True)  34.6 us
    dot_general x3, matrix products, dot_last(): lax.dot_general(left, right, (((1,), (1,)), ((), ())), preferred_element_...  21.3 us
    dot_general x3, matrix products, dot_first(): lax.dot_general(left, right, (((0,), (0,)), ((), ())), preferred_element_...  14.8 us
  transfers between devices with their start and end apart: 7, of which 6 were waited for; matrix products, arithmetic and copies ran while one was open for 32% of the time, Pallas kernels for 0%

commit v1 on v0

--- a/solution.py
+++ b/solution.py
@@ -1,6 +1,10 @@
+import functools
+
 import jax
 import jax.numpy as jnp
 from jax import lax
+from jax.experimental import pallas as pl
+from jax.experimental.pallas import tpu as pltpu
 from jax.sharding import PartitionSpec as P
 
 LAYERS = 2
@@ -84,10 +88,437 @@
     bias_grad = jnp.sum(grad_all.astype(jnp.float32), axis=0)
     return (recon_sum.astype(jnp.bfloat16), enc_grad[None], dec_grad[None], bias_grad[None])
 
+KC = 256
+DC = 128
+MESH = pl.DeviceIdType.MESH
+VMEM_LIMIT = 67043328
+BF = jnp.bfloat16
+
+
+def pick(rows, cols, stride, offset):
+    r = lax.broadcasted_iota(jnp.int32, (rows, cols), 0)
+    c = lax.broadcasted_iota(jnp.int32, (rows, cols), 1)
+    return (c == stride * r + offset).astype(BF)
+
+
+def mm(left, right):
+    return jnp.dot(left, right, preferred_element_type=jnp.float32)
+
+
+def step_kernel(
+    n, J, res, shuf, mlp, enc, dec, bias, dbias,
+    feats, xs, errs, gpre, bgrad, rebuilt,
+    enc_v, wv, raw, xsend, xg, mlpx, msend, pre_own, pre_send, pre_recv, fall,
+    nsend, nrecv, facc, osend, rrecv, e0, e1, rc, rb, g_own, g_send, g_recv, gall,
+    sem_l, sem_raw, x_s, x_r, m_s, m_r, p_s, p_r, f_s, f_r, n_s, n_r, r_s, r_r,
+    e_s, e_r, t_s, t_r, b_s, b_r, g_s, g_r, q_s, q_r,
+):
+    z = lax.axis_index("feat")
+    x = lax.axis_index("layer")
+    c = lax.axis_index("row")
+    R, H = xsend.shape[1:]
+    F = enc_v.shape[0]
+    T = xs.shape[0]
+    T2, CR, NC = T // 2, 2 * R, H // J
+    nk = F // KC
+    scale = float(T) ** (-0.5)
+    other_c, other_x = 1 - c, 1 - x
+
+    def far(dz):
+        return lax.rem(z + dz, n)
+
+    def back(dz):
+        return lax.rem(z + n - dz, n)
+
+    def remote(src, dst, send, recv, **where):
+        return pltpu.make_async_remote_copy(
+            src_ref=src, dst_ref=dst, send_sem=send, recv_sem=recv,
+            device_id=where, device_id_type=MESH)
+
+    enc_copy = pltpu.make_async_copy(enc, enc_v, sem_l)
+    enc_copy.start()
+
+    def raw_copy(i, slot):
+        return pltpu.make_async_copy(
+            dec.at[pl.ds(pl.multiple_of(i * DC, DC), DC)], raw.at[slot], sem_raw.at[slot])
+
+    raw_copy(0, 0).start()
+
+    barrier = pltpu.get_barrier_semaphore()
+    for dz in range(n):
+        if dz:
+            pl.semaphore_signal(barrier, inc=1, device_id={"feat": far(dz), "row": c}, device_id_type=MESH)
+        pl.semaphore_signal(barrier, inc=1, device_id={"feat": far(dz), "row": other_c}, device_id_type=MESH)
+    for cc in (c, other_c):
+        pl.semaphore_signal(barrier, inc=1, device_id={"layer": other_x, "row": cc}, device_id_type=MESH)
+
+    own_x = mm(pick(R, 2 * R, 2, x), res.reshape(2 * R, 2 * H)[...]).astype(BF)
+    x_mine = jnp.where(c == 0, own_x[:, :H], own_x[:, H:])
+    xsend[0] = x_mine
+    xsend[1] = jnp.where(c == 0, own_x[:, H:], own_x[:, :H])
+    xg[z, c] = x_mine
+    own_m = mm(pick(R, 2 * R, 2, x), mlp.reshape(2 * R, 2 * H)[...]).astype(BF)
+    mlpx[c] = jnp.where(c == 0, own_m[:, :H], own_m[:, H:])
+    msend[...] = jnp.where(c == 0, own_m[:, H:], own_m[:, :H])
+
+    pl.semaphore_wait(barrier, 2 * n + 1)
+
+    def x_copy(dz, k):
+        return remote(xsend.at[k], xg.at[z, c], x_s.at[dz, k], x_r.at[dz, k],
+                      feat=far(dz), row=c if k == 0 else other_c)
+
+    x_list = [(dz, k) for dz in range(n) for k in range(2) if dz or k]
+    for dz, k in x_list:
+        x_copy(dz, k).start()
+    m_copy = remote(msend, mlpx.at[c], m_s, m_r, row=other_c)
+    m_copy.start()
+
+    s0, s1 = pick(DC, 2 * DC, 2, 0), pick(DC, 2 * DC, 2, 1)
+    nd = F // DC
+
+    def split_body(i, carry):
+        slot = lax.rem(i, 2)
+
+        @pl.when(i + 1 < nd)
+        def _():
+            raw_copy(i + 1, 1 - slot).start()
+
+        raw_copy(i, slot).wait()
+        blk = raw.at[slot].reshape(2 * DC, H)[...]
+        rows = pl.ds(pl.multiple_of(i * DC, DC), DC)
+        wv[0, rows, :] = mm(s0, blk).astype(BF)
+        wv[1, rows, :] = mm(s1, blk).astype(BF)
+        return carry
+
+    lax.fori_loop(0, nd, split_body, 0)
+
+    for dz, k in x_list:
+        x_copy(dz, k).wait_recv()
+    perm = (lax.broadcasted_iota(jnp.int32, (T, T), 1) == shuf[...]).astype(BF)
+
+    def perm_body(q, carry):
+        cols = pl.ds(pl.multiple_of(q * KC, KC), KC)
+        xs[:, cols] = mm(perm, xg[:, :, :, cols].reshape(T, KC)).astype(BF)
+        return carry
+
+    lax.fori_loop(0, H // KC, perm_body, 0)
+    enc_copy.wait()
+
+    def cols_of(k):
+        return pl.ds(pl.multiple_of(k * KC, KC), KC)
+
+    def keep_and_send(v, k, own, send):
+        top, bot = v[:T2], v[T2:]
+        own[k] = jnp.where(c == 0, top, bot)
+        send[k] = jnp.where(c == 0, bot, top)
+
+    def p_copy(k):
+        return remote(pre_send.at[k], pre_recv.at[k], p_s.at[k], p_r.at[k], row=other_c)
+
+    def f_copy(k):
+        return remote(fall.at[c, k], fall.at[c, k], f_s.at[k], f_r.at[k], row=other_c)
+
+    def pre_body(k, carry):
+        keep_and_send(dot_last(xs[...], enc_v[cols_of(k), :]), k, pre_own, pre_send)
+        p_copy(k).start()
+        return carry
+
+    lax.fori_loop(0, nk, pre_body, 0)
+
+    def feat_body(k, carry):
+        p_copy(k).wait_recv()
+        v = pre_own[k] + pre_recv[k] + bias[:, cols_of(k)]
+        fall[c, k] = jnp.maximum(v, 0.0).astype(BF)
+        f_copy(k).start()
+        return carry
+
+    lax.fori_loop(0, nk, feat_body, 0)
+
+    def join_body(k, carry):
+        f_copy(k).wait_recv()
+        feats[:, cols_of(k)] = jnp.concatenate([fall[0, k], fall[1, k]], axis=0)
+        return carry
+
+    lax.fori_loop(0, nk, join_body, 0)
+
+    def n_copy(j):
+        return remote(nsend.at[j], nrecv.at[j], n_s.at[j], n_r.at[j], layer=other_x)
+
+    def r_copy(j, dz):
+        return remote(osend.at[j, far(dz)], rrecv.at[j, dz - 1], r_s.at[j, dz], r_r.at[j, dz], feat=far(dz))
+
+    def e_copy(j, dz):
+        return remote(e0.at[j, z], e0.at[j, z], e_s.at[j, dz], e_r.at[j, dz], feat=far(dz))
+
+    def t_copy(j, dz):
+        return remote(e0.at[j, back(dz)], e1.at[j, back(dz)], t_s.at[j, dz], t_r.at[j, dz], layer=other_x)
+
+    def spots(j, q):
+        wide = pl.ds(pl.multiple_of(j * NC + q * KC, KC), KC)
+        return wide, pl.ds(pl.multiple_of(q * KC, KC), KC)
+
+    @pl.when(x == 0)
+    def _():
+        for j in range(J):
+            def next_body(q, carry):
+                wide, near = spots(j, q)
+                nsend[j, :, near] = mm(feats[...], wv[1, :, wide]).astype(BF)
+                return carry
+
+            lax.fori_loop(0, NC // KC, next_body, 0)
+            n_copy(j).start()
+
+            def own_body(q, carry):
+                wide, near = spots(j, q)
+                v = mm(feats[...], wv[0, :, wide]).reshape(n, CR, KC)
+                facc[:, :, wide] = v
+                osend[j, :, :, near] = v.astype(BF)
+                return carry
+
+            lax.fori_loop(0, NC // KC, own_body, 0)
+            for dz in range(1, n):
+                r_copy(j, dz).start()
+
+    @pl.when(x == 1)
+    def _():
+        for j in range(J):
+            def own_body(q, carry):
+                wide, near = spots(j, q)
+                facc[:, :, wide] = mm(feats[...], wv[0, :, wide]).reshape(n, CR, KC)
+                return carry
+
+            lax.fori_loop(0, NC // KC, own_body, 0)
+        for j in range(J):
+            n_copy(j).wait_recv()
+
+            def add_body(q, carry):
+                wide, near = spots(j, q)
+                v = facc[:, :, wide] + nrecv[j, :, near].astype(jnp.float32).reshape(n, CR, KC)
+                facc[:, :, wide] = v
+                osend[j, :, :, near] = v.astype(BF)
+                return carry
+
+            lax.fori_loop(0, NC // KC, add_body, 0)
+            for dz in range(1, n):
+                r_copy(j, dz).start()
+
+    m_copy.wait_recv()
+
+    def reduce_chunk(j):
+        for dz in range(1, n):
+            r_copy(j, dz).wait_recv()
+        wide = pl.ds(j * NC, NC)
+        total = facc[z, :, wide]
+        for dz in range(1, n):
+            total = total + rrecv[j, dz - 1].astype(jnp.float32)
+        d = jnp.where(
+            x == 0,
+            jnp.where(c == 0, dbias[0:1, j * NC:(j + 1) * NC], dbias[0:1, H + j * NC:H + (j + 1) * NC]),
+            jnp.where(c == 0, dbias[1:2, j * NC:(j + 1) * NC], dbias[1:2, H + j * NC:H + (j + 1) * NC]))
+        total = total + d
+        e0[j, z] = (total - mlpx[:, :, wide].reshape(CR, NC).astype(jnp.float32)).astype(BF)
+        for dz in range(1, n):
+            e_copy(j, dz).start()
+
+        @pl.when(x == 1)
+        def _():
+            t_copy(j, 0).start()
+
+        rc[:, j] = total.astype(BF).reshape(2, R, NC)
+
+    def pass_chunk(j):
+        for dz in range(1, n):
+            e_copy(j, dz).wait_recv()
+
+            @pl.when(x == 1)
+            def _():
+                t_copy(j, dz).start()
+
+    for j in range(J):
+        reduce_chunk(j)
+        if j:
+            pass_chunk(j - 1)
+    pass_chunk(J - 1)
+
+    def b_copy(k):
+        dx, dc = k // 2, k % 2
+        to_x = other_x if dx else x
+        to_c = other_c if dc else c
+        return remote(rc.at[to_c], rb.at[x, c], b_s.at[k], b_r.at[k], layer=to_x, row=to_c)
+
+    for k in range(1, 4):
+        b_copy(k).start()
+    rb[x, c] = rc[c]
+
+    for j in range(J):
+        errs[0, :, j * NC:(j + 1) * NC] = e0[j].reshape(T, NC)
+
+    @pl.when(x == 0)
+    def _():
+        for j in range(J):
+            for dz in range(n):
+                t_copy(j, dz).wait_recv()
+            errs[1, :, j * NC:(j + 1) * NC] = e1[j].reshape(T, NC)
+
+    @pl.when(x == 1)
+    def _():
+        errs[1] = jnp.zeros((T, H), BF)
+
+    def g_copy(k):
+        return remote(g_send.at[k], g_recv.at[k], g_s.at[k], g_r.at[k], row=other_c)
+
+    def q_copy(k):
+        return remote(gall.at[c, k], gall.at[c, k], q_s.at[k], q_r.at[k], row=other_c)
+
+    @pl.when(x == 0)
+    def _():
+        def grad_body(k, carry):
+            v = dot_last(errs[0], wv[0, cols_of(k), :]) + dot_last(errs[1], wv[1, cols_of(k), :])
+            keep_and_send(v, k, g_own, g_send)
+            g_copy(k).start()
+            return carry
+
+        lax.fori_loop(0, nk, grad_body, 0)
+
+    @pl.when(x == 1)
+    def _():
+        def grad_body(k, carry):
+            keep_and_send(dot_last(errs[0], wv[0, cols_of(k), :]), k, g_own, g_send)
+            g_copy(k).start()
+            return carry
+
+        lax.fori_loop(0, nk, grad_body, 0)
+
+    def mask_body(k, carry):
+        g_copy(k).wait_recv()
+        v = (g_own[k] + g_recv[k]) * scale
+        gall[c, k] = jnp.where(fall[c, k].astype(jnp.float32) > 0, v, 0.0).astype(BF)
+        q_copy(k).start()
+        return carry
+
+    lax.fori_loop(0, nk, mask_body, 0)
+
+    for k in range(1, 4):
+        b_copy(k).wait_recv()
+    i0, i1 = pick(R, 2 * R, 2, 0).T, pick(R, 2 * R, 2, 1).T
+    out = rebuilt.reshape(2 * R, 2 * H)
+    for h in range(2):
+        for j in range(J):
+            lo = h * H + j * NC
+            out[:, lo:lo + NC] = (mm(i0, rb[0, h, j]) + mm(i1, rb[1, h, j])).astype(BF)
+
+    def last_body(k, carry):
+        q_copy(k).wait_recv()
+        both = jnp.concatenate([gall[0, k], gall[1, k]], axis=0)
+        gpre[:, cols_of(k)] = both
+        bgrad[:, cols_of(k)] = jnp.sum(both.astype(jnp.float32), axis=0, keepdims=True)
+        p_copy(k).wait_send()
+        f_copy(k).wait_send()
+        g_copy(k).wait_send()
+        q_copy(k).wait_send()
+        return carry
+
+    lax.fori_loop(0, nk, last_body, 0)
+
+    for dz, k in x_list:
+        x_copy(dz, k).wait_send()
+    m_copy.wait_send()
+    for j in range(J):
+        for dz in range(1, n):
+            r_copy(j, dz).wait_send()
+            e_copy(j, dz).wait_send()
+    for k in range(1, 4):
+        b_copy(k).wait_send()
+
+    @pl.when(x == 0)
+    def _():
+        for j in range(J):
+            n_copy(j).wait_send()
+
+    @pl.when(x == 1)
+    def _():
+        for j in range(J):
+            for dz in range(n):
+                t_copy(j, dz).wait_send()
+
+
+def weight_kernel(scale, feats, gpre, errs, xs, enc_grad, dec_grad):
+    fc, H = enc_grad.shape
+    f = feats[...]
+    enc_grad[...] = dot_first(gpre[...], xs[...]).astype(BF)
+    g = dot_first(mm(f, pick(fc, 2 * fc, 2, 0)).astype(BF), errs[0])
+    g = g + dot_first(mm(f, pick(fc, 2 * fc, 2, 1)).astype(BF), errs[1])
+    dec_grad.reshape(2 * fc, H)[...] = (scale * g).astype(BF)
+
+
+def fused(resid_buf, shuffle, mlp_out, enc_weight, dec_weight, enc_bias, dec_bias):
+    n = lax.axis_size("feat")
+    R = resid_buf.shape[0]
+    F, H = enc_weight.shape[1:]
+    T = R * n * 2
+    T2, CR = T // 2, 2 * R
+    J = 3 if H % (3 * KC) == 0 else 1
+    NC, nk = H // J, F // KC
+    f32 = jnp.float32
+    vm = pl.BlockSpec(memory_space=pltpu.VMEM)
+    hbm = pl.BlockSpec(memory_space=pl.ANY)
+    dma = pltpu.SemaphoreType.DMA
+    shape = jax.ShapeDtypeStruct
+    feats, xs, errs, gpre, bgrad, rebuilt = pl.pallas_call(
+        functools.partial(step_kernel, n, J),
+        out_shape=(
+            shape((T, F), BF), shape((T, H), BF), shape((2, T, H), BF), shape((T, F), BF),
+            shape((1, F), f32), shape((R, 2, 2 * H), BF)),
+        in_specs=[vm, vm, vm, hbm, hbm, vm, vm],
+        out_specs=[vm] * 6,
+        scratch_shapes=[
+            pltpu.VMEM((F, H), BF), pltpu.VMEM((2, F, H), BF), pltpu.VMEM((2, DC, 2, H), BF),
+            pltpu.VMEM((2, R, H), BF), pltpu.VMEM((n, 2, R, H), BF),
+            pltpu.VMEM((2, R, H), BF), pltpu.VMEM((R, H), BF),
+            pltpu.VMEM((nk, T2, KC), f32), pltpu.VMEM((nk, T2, KC), f32), pltpu.VMEM((nk, T2, KC), f32),
+            pltpu.VMEM((2, nk, T2, KC), BF),
+            pltpu.VMEM((J, T, NC), BF), pltpu.VMEM((J, T, NC), BF), pltpu.VMEM((n, CR, H), f32),
+            pltpu.VMEM((J, n, CR, NC), BF), pltpu.VMEM((J, n - 1, CR, NC), BF),
+            pltpu.VMEM((J, n, CR, NC), BF), pltpu.VMEM((J, n, CR, NC), BF),
+            pltpu.VMEM((2, J, R, NC), BF), pltpu.VMEM((2, 2, J, R, NC), BF),
+            pltpu.VMEM((nk, T2, KC), f32), pltpu.VMEM((nk, T2, KC), f32), pltpu.VMEM((nk, T2, KC), f32),
+            pltpu.VMEM((2, nk, T2, KC), BF),
+            dma, dma((2,)), dma((n, 2)), dma((n, 2)), dma, dma, dma((nk,)), dma((nk,)),
+            dma((nk,)), dma((nk,)), dma((J,)), dma((J,)), dma((J, n)), dma((J, n)),
+            dma((J, n)), dma((J, n)), dma((J, n)), dma((J, n)), dma((4,)), dma((4,)),
+            dma((nk,)), dma((nk,)), dma((nk,)), dma((nk,)),
+        ],
+        compiler_params=pltpu.CompilerParams(
+            collective_id=0, has_side_effects=True, vmem_limit_bytes=VMEM_LIMIT),
+    )(resid_buf, shuffle.reshape(T, 1), mlp_out, enc_weight[0], dec_weight[0], enc_bias, dec_bias)
+    fc = 128
+    enc_grad, dec_grad = pl.pallas_call(
+        functools.partial(weight_kernel, float(T) ** (-0.5)),
+        grid=(F // fc,),
+        out_shape=(shape((F, H), BF), shape((F, 2, H), BF)),
+        in_specs=[
+            pl.BlockSpec((T, fc), lambda i: (0, i)), pl.BlockSpec((T, fc), lambda i: (0, i)),
+            pl.BlockSpec((2, T, H), lambda i: (0, 0, 0)), pl.BlockSpec((T, H), lambda i: (0, 0))],
+        out_specs=(
+            pl.BlockSpec((fc, H), lambda i: (i, 0)), pl.BlockSpec((fc, 2, H), lambda i: (i, 0, 0))),
+        compiler_params=pltpu.CompilerParams(vmem_limit_bytes=VMEM_LIMIT),
+    )(feats, gpre, errs, xs)
+    return rebuilt, enc_grad[None], dec_grad[None], bgrad
+
+
+def chosen(resid_buf, shuffle, mlp_out, enc_weight, dec_weight, enc_bias, dec_bias):
+    args = (resid_buf, shuffle, mlp_out, enc_weight, dec_weight, enc_bias, dec_bias)
+    rows, width = resid_buf.shape[0], enc_weight.shape[2]
+    fits = (
+        lax.axis_size("layer") == LAYERS == 2 and lax.axis_size("row") == 2
+        and 1 < lax.axis_size("feat") <= 4 and rows % 16 == 0
+        and width % KC == 0 and enc_weight.shape[1] % KC == 0)
+    return fused(*args) if fits else on_device(*args)
+
 
 def solution(mesh):
     return jax.shard_map(
-        on_device,
+        chosen,
         mesh=mesh,
         in_specs=(
             P(("groups", "feat", "row"), None, None),

time: 530 us -> 156 us (0.29)
  the two profiles are of different devices: /device:TPU:0 before, /device:TPU:29 now
where the time goes in v1:
time: 156 us
  Pallas kernels  150 us (96%)
  local copies, waits for them, and re-layouts  5.05 us (3%)
    pallas_call x1, Pallas kernels, fused(): pl.pallas_call(functools.partial(step_kernel, n, J), out_shape=(shape((T,...  126 us
    pallas_call x1, Pallas kernels, fused(): pl.pallas_call(functools.partial(weight_kernel, float(T) ** (-0.5)), grid...  24 us
    unnamed x2, local copies, waits for them, and re-layouts  3.58 us

profile of v1, /device:TPU:29, one launch (start us, length us, event | category | flops | bytes accessed | tf_op | source)
XLA Modules:
  0.0 155.5 jit_solution(13497705908880294136)
XLA Ops:
  0.6 1.5 copy.11.shuf
  2.1 125.8 %shard_map.102 = (bf16[256,2048]{1,0:T(8,128)(2,1)}, bf16[256,2304]{1,0:T(8,128)(2,1)}, bf16[2,256,2304]{2,1,0:T(8,128)(2,1)}, bf16[256,2048]{1,0:T(8,128)(2,1)}...) custom-call(bf16[32,2,4608]{2,1,0:T(2,128)(2,1)} %res.1, s32[256,1]{1,0:T(8,128)} %copy.11.shuf, ...), custom_call_target="tpu_custom_call" | custom-call | tf_op jit(solution)/shard_map/pallas_call | solution.py:467
  127.9 24.0 %shard_map.103 = (bf16[2048,2304]{1,0:T(8,128)(2,1)}, bf16[2048,2,2304]{2,1,0:T(2,128)(2,1)}) custom-call(bf16[256,2048]{1,0:T(8,128)(2,1)} %get-tuple-element.13.feats, bf16[256,2048]{1,0:T(8,128)(2,1)} %get-tuple-element.14.gpre, bf16[2,256,2304]{2,1,0:T(8,128)(2,1)} %get-tuple-element.15.errs, bf16[256,2304]{1,0:T(8,128)(2,1)} %get-tuple-element.16.xs), custom_call_target="tpu_custom_call" | custom-call | tf_op jit(solution)/shard_map/pallas_call | solution.py:495
  151.9 2.3 %copy.14 = bf16[32,2,4608]{2,1,0:T(2,128)(2,1)} copy(bf16[32,2,4608]{2,1,0:T(2,128)(2,1)} %get-tuple-element.24) | data formatting | bytes 1179648
  154.2 1.3 copy.15

commit v2 on v1

--- a/solution.py
+++ b/solution.py
@@ -107,7 +107,7 @@
 
 def step_kernel(
     n, J, res, shuf, mlp, enc, dec, bias, dbias,
-    feats, xs, errs, gpre, bgrad, rebuilt,
+    feats, xs, errs, gpre, parts,
     enc_v, wv, raw, xsend, xg, mlpx, msend, pre_own, pre_send, pre_recv, fall,
     nsend, nrecv, facc, osend, rrecv, e0, e1, rc, rb, g_own, g_send, g_recv, gall,
     sem_l, sem_raw, x_s, x_r, m_s, m_r, p_s, p_r, f_s, f_r, n_s, n_r, r_s, r_r,
@@ -194,11 +194,11 @@
 
     for dz, k in x_list:
         x_copy(dz, k).wait_recv()
-    perm = (lax.broadcasted_iota(jnp.int32, (T, T), 1) == shuf[...]).astype(BF)
+    perm = (lax.broadcasted_iota(jnp.int32, (T, T), 0) == shuf[...]).astype(BF)
 
     def perm_body(q, carry):
         cols = pl.ds(pl.multiple_of(q * KC, KC), KC)
-        xs[:, cols] = mm(perm, xg[:, :, :, cols].reshape(T, KC)).astype(BF)
+        xs[:, cols] = dot_first(perm, xg[:, :, :, cols].reshape(T, KC)).astype(BF)
         return carry
 
     lax.fori_loop(0, H // KC, perm_body, 0)
@@ -400,18 +400,15 @@
 
     for k in range(1, 4):
         b_copy(k).wait_recv()
-    i0, i1 = pick(R, 2 * R, 2, 0).T, pick(R, 2 * R, 2, 1).T
-    out = rebuilt.reshape(2 * R, 2 * H)
     for h in range(2):
         for j in range(J):
             lo = h * H + j * NC
-            out[:, lo:lo + NC] = (mm(i0, rb[0, h, j]) + mm(i1, rb[1, h, j])).astype(BF)
+            parts[:, lo:lo + NC] = rb[:, h, j].reshape(2 * R, NC)
 
     def last_body(k, carry):
         q_copy(k).wait_recv()
         both = jnp.concatenate([gall[0, k], gall[1, k]], axis=0)
         gpre[:, cols_of(k)] = both
-        bgrad[:, cols_of(k)] = jnp.sum(both.astype(jnp.float32), axis=0, keepdims=True)
         p_copy(k).wait_send()
         f_copy(k).wait_send()
         g_copy(k).wait_send()
@@ -442,13 +439,25 @@
                 t_copy(j, dz).wait_send()
 
 
-def weight_kernel(scale, feats, gpre, errs, xs, enc_grad, dec_grad):
+def weight_kernel(scale, feats, gpre, errs, xs, parts, enc_grad, dec_grad, bgrad, rebuilt):
     fc, H = enc_grad.shape
-    f = feats[...]
+    R2 = parts.shape[0]
+
+    @pl.when(pl.program_id(0) == 0)
+    def _():
+        i = lax.broadcasted_iota(jnp.int32, (R2, R2), 0)
+        j = lax.broadcasted_iota(jnp.int32, (R2, R2), 1)
+        inter = (j == (i % 2) * (R2 // 2) + i // 2).astype(BF)
+        rebuilt.reshape(R2, 2 * H)[...] = mm(inter, parts[...]).astype(BF)
+
+    bgrad[...] = jnp.sum(gpre[...].astype(jnp.float32), axis=0, keepdims=True)
     enc_grad[...] = dot_first(gpre[...], xs[...]).astype(BF)
-    g = dot_first(mm(f, pick(fc, 2 * fc, 2, 0)).astype(BF), errs[0])
-    g = g + dot_first(mm(f, pick(fc, 2 * fc, 2, 1)).astype(BF), errs[1])
-    dec_grad.reshape(2 * fc, H)[...] = (scale * g).astype(BF)
+    p0, p1 = pick(DC, 2 * DC, 2, 0), pick(DC, 2 * DC, 2, 1)
+    out = dec_grad.reshape(2 * fc, H)
+    for b in range(fc // DC):
+        f = feats[:, b * DC:(b + 1) * DC]
+        g = dot_first(mm(f, p0).astype(BF), errs[0]) + dot_first(mm(f, p1).astype(BF), errs[1])
+        out[b * 2 * DC:(b + 1) * 2 * DC, :] = (scale * g).astype(BF)
 
 
 def fused(resid_buf, shuffle, mlp_out, enc_weight, dec_weight, enc_bias, dec_bias):
@@ -457,20 +466,20 @@
     F, H = enc_weight.shape[1:]
     T = R * n * 2
     T2, CR = T // 2, 2 * R
-    J = 3 if H % (3 * KC) == 0 else 1
+    J = H // KC
     NC, nk = H // J, F // KC
     f32 = jnp.float32
     vm = pl.BlockSpec(memory_space=pltpu.VMEM)
     hbm = pl.BlockSpec(memory_space=pl.ANY)
     dma = pltpu.SemaphoreType.DMA
     shape = jax.ShapeDtypeStruct
-    feats, xs, errs, gpre, bgrad, rebuilt = pl.pallas_call(
+    feats, xs, errs, gpre, parts = pl.pallas_call(
         functools.partial(step_kernel, n, J),
         out_shape=(
             shape((T, F), BF), shape((T, H), BF), shape((2, T, H), BF), shape((T, F), BF),
-            shape((1, F), f32), shape((R, 2, 2 * H), BF)),
+            shape((2 * R, 2 * H), BF)),
         in_specs=[vm, vm, vm, hbm, hbm, vm, vm],
-        out_specs=[vm] * 6,
+        out_specs=[vm] * 5,
         scratch_shapes=[
             pltpu.VMEM((F, H), BF), pltpu.VMEM((2, F, H), BF), pltpu.VMEM((2, DC, 2, H), BF),
             pltpu.VMEM((2, R, H), BF), pltpu.VMEM((n, 2, R, H), BF),
@@ -490,19 +499,22 @@
         ],
         compiler_params=pltpu.CompilerParams(
             collective_id=0, has_side_effects=True, vmem_limit_bytes=VMEM_LIMIT),
-    )(resid_buf, shuffle.reshape(T, 1), mlp_out, enc_weight[0], dec_weight[0], enc_bias, dec_bias)
-    fc = 128
-    enc_grad, dec_grad = pl.pallas_call(
+    )(resid_buf, shuffle.reshape(1, T), mlp_out, enc_weight[0], dec_weight[0], enc_bias, dec_bias)
+    fc = 512 if F % 512 == 0 else KC
+    enc_grad, dec_grad, bgrad, rebuilt = pl.pallas_call(
         functools.partial(weight_kernel, float(T) ** (-0.5)),
         grid=(F // fc,),
-        out_shape=(shape((F, H), BF), shape((F, 2, H), BF)),
+        out_shape=(
+            shape((F, H), BF), shape((F, 2, H), BF), shape((1, F), f32), shape((R, 2, 2 * H), BF)),
         in_specs=[
             pl.BlockSpec((T, fc), lambda i: (0, i)), pl.BlockSpec((T, fc), lambda i: (0, i)),
-            pl.BlockSpec((2, T, H), lambda i: (0, 0, 0)), pl.BlockSpec((T, H), lambda i: (0, 0))],
+            pl.BlockSpec((2, T, H), lambda i: (0, 0, 0)), pl.BlockSpec((T, H), lambda i: (0, 0)),
+            pl.BlockSpec((2 * R, 2 * H), lambda i: (0, 0))],
         out_specs=(
-            pl.BlockSpec((fc, H), lambda i: (i, 0)), pl.BlockSpec((fc, 2, H), lambda i: (i, 0, 0))),
+            pl.BlockSpec((fc, H), lambda i: (i, 0)), pl.BlockSpec((fc, 2, H), lambda i: (i, 0, 0)),
+            pl.BlockSpec((1, fc), lambda i: (0, i)), pl.BlockSpec((R, 2, 2 * H), lambda i: (0, 0, 0))),
         compiler_params=pltpu.CompilerParams(vmem_limit_bytes=VMEM_LIMIT),
-    )(feats, gpre, errs, xs)
+    )(feats, gpre, errs, xs, parts)
     return rebuilt, enc_grad[None], dec_grad[None], bgrad
 
 

time: 156 us -> 142 us (0.910)
  the two profiles are of different devices: /device:TPU:29 before, /device:TPU:0 now
where the time goes in v2:
time: 142 us; the launch traced here: 141 us
  Pallas kernels  141 us (99%)
    pallas_call x1, Pallas kernels, fused(): pl.pallas_call(functools.partial(step_kernel, n, J), out_shape=(shape((T,...  118 us
    pallas_call x1, Pallas kernels, fused(): pl.pallas_call(functools.partial(weight_kernel, float(T) ** (-0.5)), grid...  22.7 us

profile of v2, /device:TPU:0, one launch (start us, length us, event | category | flops | bytes accessed | tf_op | source)
XLA Modules:
  0.0 141.2 jit_solution(2793232713378428285)
XLA Ops:
  0.6 117.8 %shard_map.102 = (bf16[256,2048]{1,0:T(8,128)(2,1)}, bf16[256,2304]{1,0:T(8,128)(2,1)}, bf16[2,256,2304]{2,1,0:T(8,128)(2,1)}, bf16[256,2048]{1,0:T(8,128)(2,1)}, bf16[64,4608]{1,0:T(8,128)(2,1)}) custom-call(bf16[32,2,4608]{2,1,0:T(2,128)(2,1)} %res.1, s32[1,256]{1,0:T(1,128)} %bitcast.7, bf16[32,2,4608]{2,1,0:T(2,128)(2,1)} %mlp.1, ...), custom_call_target="tpu_custom_call" | custom-call | tf_op jit(solution)/shard_map/pallas_call | solution.py:476
  118.4 22.7 %shard_map.103 = (bf16[2048,2304]{1,0:T(8,128)(2,1)}, bf16[2048,2,2304]{2,1,0:T(2,128)(2,1)}, f32[1,2048]{1,0:T(1,128)}, bf16[32,2,4608]{2,1,0:T(2,128)(2,1)}) custom-call(bf16[256,2048]{1,0:T(8,128)(2,1)} %get-tuple-element.13.feats, bf16[256,2048]{1,0:T(8,128)(2,1)} %get-tuple-element.14.gpre, bf16[2,256,2304]{2,1,0:T(8,128)(2,1)} %get-tuple-element.15.errs, ...), custom_call_target="tpu_custom_call" | custom-call | tf_op jit(solution)/shard_map/pallas_call | solution.py:504

commit v3 on v2

--- a/solution.py
+++ b/solution.py
@@ -111,7 +111,7 @@
     enc_v, wv, raw, xsend, xg, mlpx, msend, pre_own, pre_send, pre_recv, fall,
     nsend, nrecv, facc, osend, rrecv, e0, e1, rc, rb, g_own, g_send, g_recv, gall,
     sem_l, sem_raw, x_s, x_r, m_s, m_r, p_s, p_r, f_s, f_r, n_s, n_r, r_s, r_r,
-    e_s, e_r, t_s, t_r, b_s, b_r, g_s, g_r, q_s, q_r,
+    e_s, e_r, t_s, t_r, b_s, b_r, g_s, g_r, q_s, q_r, y_s, w_s,
 ):
     z = lax.axis_index("feat")
     x = lax.axis_index("layer")
@@ -135,6 +135,23 @@
             src_ref=src, dst_ref=dst, send_sem=send, recv_sem=recv,
             device_id=where, device_id_type=MESH)
 
+    line = n == 4
+
+    def unless_ends(dz, act):
+        if line and dz == n - 1:
+            pl.when(z != 0)(act)
+        elif line and dz == 1:
+            pl.when(z != n - 1)(act)
+        else:
+            act()
+
+    def relays(act):
+        if line:
+            pl.when(z == 2)(lambda: act(1, 3))
+            pl.when(z == 1)(lambda: act(3, 1))
+
+    orders = (2, 1, 3) if line else tuple(range(1, n))
+
     enc_copy = pltpu.make_async_copy(enc, enc_v, sem_l)
     enc_copy.start()
 
@@ -167,9 +184,14 @@
         return remote(xsend.at[k], xg.at[z, c], x_s.at[dz, k], x_r.at[dz, k],
                       feat=far(dz), row=c if k == 0 else other_c)
 
-    x_list = [(dz, k) for dz in range(n) for k in range(2) if dz or k]
+    x_list = [(dz, k) for dz in orders for k in range(2)] + [(0, 1)]
     for dz, k in x_list:
-        x_copy(dz, k).start()
+        unless_ends(dz, lambda: x_copy(dz, k).start())
+
+    def y_copy(k, to, at):
+        cc = c if k == 0 else other_c
+        return remote(xg.at[back(2), cc], xg.at[back(2), cc], y_s.at[k], x_r.at[at, k], feat=far(to))
+
     m_copy = remote(msend, mlpx.at[c], m_s, m_r, row=other_c)
     m_copy.start()
 
@@ -190,10 +212,16 @@
         wv[1, rows, :] = mm(s1, blk).astype(BF)
         return carry
 
-    lax.fori_loop(0, nd, split_body, 0)
+    lax.fori_loop(0, nd // 2, split_body, 0)
+    if line:
+        for k in range(2):
+            x_copy(2, k).wait_recv()
+            relays(lambda to, at: y_copy(k, to, at).start())
+    lax.fori_loop(nd // 2, nd, split_body, 0)
 
     for dz, k in x_list:
-        x_copy(dz, k).wait_recv()
+        if not line or dz != 2:
+            x_copy(dz, k).wait_recv()
     perm = (lax.broadcasted_iota(jnp.int32, (T, T), 0) == shuf[...]).astype(BF)
 
     def perm_body(q, carry):
@@ -249,6 +277,9 @@
 
     def e_copy(j, dz):
         return remote(e0.at[j, z], e0.at[j, z], e_s.at[j, dz], e_r.at[j, dz], feat=far(dz))
+
+    def w_copy(j, to, at):
+        return remote(e0.at[j, back(2)], e0.at[j, back(2)], w_s.at[j], e_r.at[j, at], feat=far(to))
 
     def t_copy(j, dz):
         return remote(e0.at[j, back(dz)], e1.at[j, back(dz)], t_s.at[j, dz], t_r.at[j, dz], layer=other_x)
@@ -317,8 +348,8 @@
             jnp.where(c == 0, dbias[1:2, j * NC:(j + 1) * NC], dbias[1:2, H + j * NC:H + (j + 1) * NC]))
         total = total + d
         e0[j, z] = (total - mlpx[:, :, wide].reshape(CR, NC).astype(jnp.float32)).astype(BF)
-        for dz in range(1, n):
-            e_copy(j, dz).start()
+        for dz in orders:
+            unless_ends(dz, lambda: e_copy(j, dz).start())
 
         @pl.when(x == 1)
         def _():
@@ -327,8 +358,10 @@
         rc[:, j] = total.astype(BF).reshape(2, R, NC)
 
     def pass_chunk(j):
-        for dz in range(1, n):
+        for dz in orders:
             e_copy(j, dz).wait_recv()
+            if line and dz == 2:
+                relays(lambda to, at: w_copy(j, to, at).start())
 
             @pl.when(x == 1)
             def _():
@@ -418,12 +451,16 @@
     lax.fori_loop(0, nk, last_body, 0)
 
     for dz, k in x_list:
-        x_copy(dz, k).wait_send()
+        unless_ends(dz, lambda: x_copy(dz, k).wait_send())
+    for k in range(2):
+        relays(lambda to, at: y_copy(k, to, at).wait_send())
+    for j in range(J):
+        relays(lambda to, at: w_copy(j, to, at).wait_send())
     m_copy.wait_send()
     for j in range(J):
         for dz in range(1, n):
             r_copy(j, dz).wait_send()
-            e_copy(j, dz).wait_send()
+            unless_ends(dz, lambda: e_copy(j, dz).wait_send())
     for k in range(1, 4):
         b_copy(k).wait_send()
 
@@ -495,7 +532,7 @@
             dma, dma((2,)), dma((n, 2)), dma((n, 2)), dma, dma, dma((nk,)), dma((nk,)),
             dma((nk,)), dma((nk,)), dma((J,)), dma((J,)), dma((J, n)), dma((J, n)),
             dma((J, n)), dma((J, n)), dma((J, n)), dma((J, n)), dma((4,)), dma((4,)),
-            dma((nk,)), dma((nk,)), dma((nk,)), dma((nk,)),
+            dma((nk,)), dma((nk,)), dma((nk,)), dma((nk,)), dma((2,)), dma((J,)),
         ],
         compiler_params=pltpu.CompilerParams(
             collective_id=0, has_side_effects=True, vmem_limit_bytes=VMEM_LIMIT),

time: 142 us -> 141 us (level)
  no operation moved by 1% of the time
where the time goes in v3:
time: 141 us
  Pallas kernels  140 us (99%)
    pallas_call x1, Pallas kernels, fused(): pl.pallas_call(functools.partial(step_kernel, n, J), out_shape=(shape((T,...  117 us
    pallas_call x1, Pallas kernels, fused(): pl.pallas_call(functools.partial(weight_kernel, float(T) ** (-0.5)), grid...  22.7 us

profile of v3, /device:TPU:0, one launch (start us, length us, event | category | flops | bytes accessed | tf_op | source)
XLA Modules:
  0.0 140.7 jit_solution(2300013410186326907)
XLA Ops:
  0.6 117.3 %shard_map.102 = (bf16[256,2048]{1,0:T(8,128)(2,1)}, bf16[256,2304]{1,0:T(8,128)(2,1)}, bf16[2,256,2304]{2,1,0:T(8,128)(2,1)}, bf16[256,2048]{1,0:T(8,128)(2,1)}, bf16[64,4608]{1,0:T(8,128)(2,1)}) custom-call(bf16[32,2,4608]{2,1,0:T(2,128)(2,1)} %res.1, s32[1,256]{1,0:T(1,128)} %bitcast.7, bf16[32,2,4608]{2,1,0:T(2,128)(2,1)} %mlp.1, ...), custom_call_target="tpu_custom_call" | custom-call | tf_op jit(solution)/shard_map/pallas_call | solution.py:513
  117.9 22.7 %shard_map.103 = (bf16[2048,2304]{1,0:T(8,128)(2,1)}, bf16[2048,2,2304]{2,1,0:T(2,128)(2,1)}, f32[1,2048]{1,0:T(1,128)}, bf16[32,2,4608]{2,1,0:T(2,128)(2,1)}) custom-call(bf16[256,2048]{1,0:T(8,128)(2,1)} %get-tuple-element.13.feats, bf16[256,2048]{1,0:T(8,128)(2,1)} %get-tuple-element.14.gpre, bf16[2,256,2304]{2,1,0:T(8,128)(2,1)} %get-tuple-element.15.errs, ...), custom_call_target="tpu_custom_call" | custom-call | tf_op jit(solution)/shard_map/pallas_call | solution.py:541

commit v4 on v3

--- a/solution.py
+++ b/solution.py
@@ -157,7 +157,7 @@
 
     def raw_copy(i, slot):
         return pltpu.make_async_copy(
-            dec.at[pl.ds(pl.multiple_of(i * DC, DC), DC)], raw.at[slot], sem_raw.at[slot])
+            dec.reshape(2 * F, H).at[pl.ds(pl.multiple_of(i * 2 * DC, 2 * DC), 2 * DC)], raw.at[slot], sem_raw.at[slot])
 
     raw_copy(0, 0).start()
 
@@ -195,7 +195,7 @@
     m_copy = remote(msend, mlpx.at[c], m_s, m_r, row=other_c)
     m_copy.start()
 
-    s0, s1 = pick(DC, 2 * DC, 2, 0), pick(DC, 2 * DC, 2, 1)
+    apart = jnp.concatenate([pick(DC, 2 * DC, 2, 0), pick(DC, 2 * DC, 2, 1)], axis=0)
     nd = F // DC
 
     def split_body(i, carry):
@@ -206,10 +206,10 @@
             raw_copy(i + 1, 1 - slot).start()
 
         raw_copy(i, slot).wait()
-        blk = raw.at[slot].reshape(2 * DC, H)[...]
+        both = mm(apart, raw[slot]).astype(BF)
         rows = pl.ds(pl.multiple_of(i * DC, DC), DC)
-        wv[0, rows, :] = mm(s0, blk).astype(BF)
-        wv[1, rows, :] = mm(s1, blk).astype(BF)
+        wv[0, rows, :] = both[:DC]
+        wv[1, rows, :] = both[DC:]
         return carry
 
     lax.fori_loop(0, nd // 2, split_body, 0)
@@ -518,7 +518,7 @@
         in_specs=[vm, vm, vm, hbm, hbm, vm, vm],
         out_specs=[vm] * 5,
         scratch_shapes=[
-            pltpu.VMEM((F, H), BF), pltpu.VMEM((2, F, H), BF), pltpu.VMEM((2, DC, 2, H), BF),
+            pltpu.VMEM((F, H), BF), pltpu.VMEM((2, F, H), BF), pltpu.VMEM((2, 2 * DC, H), BF),
             pltpu.VMEM((2, R, H), BF), pltpu.VMEM((n, 2, R, H), BF),
             pltpu.VMEM((2, R, H), BF), pltpu.VMEM((R, H), BF),
             pltpu.VMEM((nk, T2, KC), f32), pltpu.VMEM((nk, T2, KC), f32), pltpu.VMEM((nk, T2, KC), f32),

time: 141 us -> 141 us (level)
  no operation moved by 1% of the time
where the time goes in v4:
time: 141 us; the launch traced here: 140 us
  Pallas kernels  140 us (99%)
    pallas_call x1, Pallas kernels, fused(): pl.pallas_call(functools.partial(step_kernel, n, J), out_shape=(shape((T,...  117 us
    pallas_call x1, Pallas kernels, fused(): pl.pallas_call(functools.partial(weight_kernel, float(T) ** (-0.5)), grid...  22.7 us

profile of v4, /device:TPU:0, one launch (start us, length us, event | category | flops | bytes accessed | tf_op | source)
XLA Modules:
  0.0 140.5 jit_solution(17272379841914600845)
XLA Ops:
  0.6 117.1 %shard_map.102 = (bf16[256,2048]{1,0:T(8,128)(2,1)}, bf16[256,2304]{1,0:T(8,128)(2,1)}, bf16[2,256,2304]{2,1,0:T(8,128)(2,1)}, bf16[256,2048]{1,0:T(8,128)(2,1)}, bf16[64,4608]{1,0:T(8,128)(2,1)}) custom-call(bf16[32,2,4608]{2,1,0:T(2,128)(2,1)} %res.1, s32[1,256]{1,0:T(1,128)} %bitcast.7, bf16[32,2,4608]{2,1,0:T(2,128)(2,1)} %mlp.1, ...), custom_call_target="tpu_custom_call" | custom-call | tf_op jit(solution)/shard_map/pallas_call | solution.py:513
  117.7 22.7 %shard_map.103 = (bf16[2048,2304]{1,0:T(8,128)(2,1)}, bf16[2048,2,2304]{2,1,0:T(2,128)(2,1)}, f32[1,2048]{1,0:T(1,128)}, bf16[32,2,4608]{2,1,0:T(2,128)(2,1)}) custom-call(bf16[256,2048]{1,0:T(8,128)(2,1)} %get-tuple-element.13.feats, bf16[256,2048]{1,0:T(8,128)(2,1)} %get-tuple-element.14.gpre, bf16[2,256,2304]{2,1,0:T(8,128)(2,1)} %get-tuple-element.15.errs, ...), custom_call_target="tpu_custom_call" | custom-call | tf_op jit(solution)/shard_map/pallas_call | solution.py:541
